TPU v7x, 32 devices: a whole 2x2x4 slice. The times are simulated.
32 devices in a mesh: pair: 4 (over x, core), blk: 8 (over z, y).
Axes of the slice: x: 2, y: 2, z: 4, core: 2. Of those that a mesh axis runs over, the one named last changes fastest.
Arguments:
- left_feats: bfloat16 [4, 64, 256, 256], P('pair', None, 'blk'), may hold values from -6 to 6
- right_feats: bfloat16 [4, 64, 256, 256], P('pair', None, 'blk'), may hold values from -6 to 6
- offsets: int32 [8], P('blk'), may hold values from 0 to 3, as said below
- hidden: bfloat16 [4, 64, 256, 128], P('pair', None, 'blk'), may hold values from -1 to 1
- context: bfloat16 [4, 3, 64, 256, 128], P('pair', None, None, 'blk'), may hold values from -6 to 6
- gru_weights: bfloat16 [2, 3, 5, 164, 128], replicated, may hold values from -0.21875 to 0.21875
- hidden_grad: float32 [4, 64, 256, 128], P('pair', None, 'blk'), may hold values from -0.06 to 0.06
Outputs:
- new_hidden: bfloat16 [4, 64, 256, 128], P('pair', None, 'blk')
- weight_grads: float32 [2, 3, 5, 164, 128], replicated
- hidden_in_grad: float32 [4, 64, 256, 128], P('pair', None, 'blk')
Inputs may be any that keep to these rules, and one draw needn't show every extreme that they name: Stripe s reads the frame-2 blocks s - offsets[s] - 1 and s - offsets[s]; some stripe has offset 4 - 1.
All inputs are finite; a program needn't handle non-finite values.
Results may differ from a plain program's by a relative error of at most 0.0054.
Values may be sent and summed in bfloat16 or wider, within the bound.
A program may use at most 128 MiB of HBM per device.

v0:
```python
import functools
import math
import jax
import jax.numpy as jnp
import numpy as np
from jax import lax
from jax.sharding import PartitionSpec as P

LEVELS = 4
RADIUS = 4


def with_halo(block, sides, width):
    for axis, dim in sides:
        count = lax.axis_size(axis)
        forward = [(i, i + 1) for i in range(count - 1)]
        backward = [(target, source) for source, target in forward]
        low = lax.ppermute(
            lax.slice_in_dim(block, block.shape[dim] - width, None, axis=dim), axis, forward
        )
        high = lax.ppermute(lax.slice_in_dim(block, 0, width, axis=dim), axis, backward)
        block = jnp.concatenate([low, block, high], axis=dim)
    return block


def lookup_table(column_count, level_count, radius_len):
    tap_count = 2 * radius_len + 1
    lookup = np.zeros((column_count, 2 * column_count, level_count * tap_count), np.float32)
    positions = np.arange(column_count)
    for level_id in range(level_count):
        pool_span = 2**level_id
        pooled_cols = 2 * column_count // pool_span
        for tap_id in range(tap_count):
            centre = (positions + column_count // 2) // pool_span + tap_id - radius_len
            inside = (centre >= 0) & (centre < pooled_cols)
            for inner_id in range(pool_span):
                lookup[
                    positions[inside],
                    centre[inside] * pool_span + inner_id,
                    level_id * tap_count + tap_id,
                ] = (1.0 / pool_span)
    return lookup


def tap_stack(padded, extent, axis_dim, kernel_len):
    return jnp.concatenate(
        [
            lax.slice_in_dim(padded, tap_id, tap_id + extent, axis=axis_dim)
            for tap_id in range(kernel_len)
        ],
        axis=-1,
    )


def conv_apply(padded, weight_taps, extent, axis_dim):
    kernel_len, in_chan, out_chan = weight_taps.shape
    stacked = tap_stack(padded, extent, axis_dim, kernel_len)
    flat_taps = stacked.reshape(-1, kernel_len * in_chan)
    result = jnp.dot(
        flat_taps,
        weight_taps.reshape(kernel_len * in_chan, out_chan),
        preferred_element_type=jnp.float32,
    )
    return result.reshape(stacked.shape[:-1] + (out_chan,))


def conv_weight_grad(padded, deltas, axis_dim):
    extent = deltas.shape[axis_dim]
    kernel_len = padded.shape[axis_dim] - extent + 1
    stacked = tap_stack(padded, extent, axis_dim, kernel_len)
    flat_taps = stacked.reshape(-1, stacked.shape[-1])
    flat_deltas = deltas.reshape(-1, deltas.shape[-1])
    result = lax.dot_general(
        flat_taps, flat_deltas, (((0,), (0,)), ((), ())), preferred_element_type=jnp.float32
    )
    return result.reshape(kernel_len, padded.shape[-1], deltas.shape[-1])


def conv_input_grad(deltas, weight_taps, axis_dim):
    kernel_len, in_chan, out_chan = weight_taps.shape
    backward_taps = lax.dot_general(
        deltas.reshape(-1, out_chan),
        weight_taps.reshape(kernel_len * in_chan, out_chan),
        (((1,), (1,)), ((), ())),
        preferred_element_type=jnp.float32,
    )
    backward_taps = backward_taps.reshape(deltas.shape[:-1] + (kernel_len * in_chan,))
    summed = None
    for tap_id in range(kernel_len):
        tap_part = backward_taps[..., tap_id * in_chan : (tap_id + 1) * in_chan]
        widths = [(0, 0)] * deltas.ndim
        widths[axis_dim] = (tap_id, kernel_len - 1 - tap_id)
        shifted = jnp.pad(tap_part, widths)
        summed = shifted if summed is None else summed + shifted
    return summed


def pad_along(values, axis_dim):
    widths = [(0, 0)] * values.ndim
    widths[axis_dim] = (2, 2)
    return jnp.pad(values, widths)


def crop_along(values, axis_dim):
    extent = values.shape[axis_dim] - 4
    return lax.slice_in_dim(values, 2, extent + 2, axis=axis_dim)


def section_forward(padded, context_parts, weights, axis_dim, extend):
    extent = padded.shape[axis_dim] - 4
    hidden_width = weights.shape[-1]
    own_inputs = lax.slice_in_dim(padded, 2, extent + 2, axis=axis_dim)
    hidden_own = own_inputs[..., :hidden_width].astype(jnp.float32)
    feat_padded = padded[..., hidden_width:]
    update_gate = jax.nn.sigmoid(
        conv_apply(padded, weights[0], extent, axis_dim) + context_parts[0].astype(jnp.float32)
    )
    reset_gate = jax.nn.sigmoid(
        conv_apply(padded, weights[1], extent, axis_dim) + context_parts[1].astype(jnp.float32)
    )
    reset_hidden = (reset_gate * hidden_own).astype(jnp.bfloat16)
    gated_padded = jnp.concatenate([extend(reset_hidden), feat_padded], axis=-1)
    candidate = jnp.tanh(
        conv_apply(gated_padded, weights[2], extent, axis_dim)
        + context_parts[2].astype(jnp.float32)
    )
    blended = (1.0 - update_gate) * hidden_own + update_gate * candidate
    return (blended, (update_gate, reset_gate, candidate, hidden_own, padded, gated_padded))


def section_backward(cotangent, stored, weights, axis_dim, fold_rims):
    update_gate, reset_gate, candidate, hidden_own, padded, gated_padded = stored
    hidden_width = weights.shape[-1]
    delta_cand = (cotangent * update_gate * (1.0 - candidate * candidate)).astype(jnp.bfloat16)
    grad_cand = conv_weight_grad(gated_padded, delta_cand, axis_dim)
    back_gated = fold_rims(conv_input_grad(delta_cand, weights[2][:, :hidden_width], axis_dim))
    delta_update = (
        cotangent * (candidate - hidden_own) * update_gate * (1.0 - update_gate)
    ).astype(jnp.bfloat16)
    delta_reset = (back_gated * hidden_own * reset_gate * (1.0 - reset_gate)).astype(jnp.bfloat16)
    grad_update = conv_weight_grad(padded, delta_update, axis_dim)
    grad_reset = conv_weight_grad(padded, delta_reset, axis_dim)
    grad_stack = jnp.stack([grad_update, grad_reset, grad_cand])
    back_inputs = conv_input_grad(
        delta_update, weights[0][:, :hidden_width], axis_dim
    ) + conv_input_grad(delta_reset, weights[1][:, :hidden_width], axis_dim)
    hidden_back = cotangent * (1.0 - update_gate) + back_gated * reset_gate + fold_rims(back_inputs)
    return (grad_stack, hidden_back)


def extend_gated(values):
    return with_halo(values, (("blk", 1),), 2)


def stripe_rims(values):
    extent = values.shape[1] - 4
    edge_terms = jnp.concatenate([values[:, :2], values[:, extent + 2 :]], axis=1)
    arrived = with_halo(edge_terms, (("blk", 1),), 2)
    own_terms = values[:, 2 : extent + 2]
    from_left = jnp.pad(arrived[:, :2], ((0, 0), (0, extent - 2), (0, 0)))
    from_right = jnp.pad(arrived[:, 6:], ((0, 0), (extent - 2, 0), (0, 0)))
    return own_terms + from_left + from_right


def on_device(left_feats, right_feats, offsets, hidden, context, gru_weights, hidden_grad):
    left_block = left_feats[0]
    right_block = right_feats[0]
    offset = offsets[0]
    stripe = lax.axis_index("blk")
    column_count = left_block.shape[1]
    empty_block = jnp.zeros_like(right_block)
    low_id = stripe - offset - 1
    high_id = stripe - offset
    shards = lax.all_gather(right_block, "blk", axis=1, tiled=True)
    shard_cols = shards.shape[1]

    def pick_one(slot_block, block_id):
        local_col = block_id * column_count
        usable = (local_col >= 0) & (local_col + column_count <= shard_cols)
        picked = lax.dynamic_slice_in_dim(
            shards, jnp.clip(local_col, 0, shard_cols - column_count), column_count, 1
        )
        return jnp.where(usable, picked, slot_block)

    low_block = pick_one(empty_block, low_id)
    high_block = pick_one(empty_block, high_id)
    window = jnp.concatenate([low_block, high_block], axis=1)
    scores = jnp.einsum("hxc,hjc->hxj", left_block, window, preferred_element_type=jnp.float32) * (
        1.0 / math.sqrt(left_block.shape[-1])
    )
    lookup = jnp.asarray(lookup_table(column_count, LEVELS, RADIUS))
    features = jnp.einsum("hxj,xjf->hxf", scores, lookup, precision=lax.Precision.HIGHEST).astype(
        jnp.bfloat16
    )
    context_parts = context[0]
    first_inputs = jnp.concatenate([hidden[0], features], axis=-1)
    first_padded = with_halo(first_inputs, (("blk", 1),), 2)
    first_new, first_stored = section_forward(
        first_padded, context_parts, gru_weights[0], 1, extend_gated
    )
    first_hidden = first_new.astype(jnp.bfloat16)
    second_inputs = jnp.concatenate([first_hidden, features], axis=-1)
    second_new, second_stored = section_forward(
        pad_along(second_inputs, 0),
        context_parts,
        gru_weights[1],
        0,
        functools.partial(pad_along, axis_dim=0),
    )
    second_grads, first_back = section_backward(
        hidden_grad[0], second_stored, gru_weights[1], 0, functools.partial(crop_along, axis_dim=0)
    )
    first_grads, hidden_back = section_backward(
        first_back, first_stored, gru_weights[0], 1, stripe_rims
    )
    grad_stack = lax.psum(jnp.stack([first_grads, second_grads]), ("pair", "blk"))
    return (second_new.astype(jnp.bfloat16)[None], grad_stack, hidden_back[None])


def solution(mesh):
    placed = (
        P("pair", None, "blk", None),
        P("pair", None, "blk", None),
        P("blk"),
        P("pair", None, "blk", None),
        P("pair", None, None, "blk", None),
        P(),
        P("pair", None, "blk", None),
    )
    return jax.shard_map(
        on_device,
        mesh=mesh,
        in_specs=placed,
        out_specs=(P("pair", None, "blk", None), P(), P("pair", None, "blk", None)),
        check_vma=False,
    )
```

profile of v0, /device:TPU:0, one launch (start us, length us, event | category | flops | bytes accessed | tf_op | source)
XLA Modules:
  0.0 494.4 jit_solution(1043420342084576107)
XLA Ops:
  8.6 129.2 %all-gather.3.cloned.1.call-done = bf16[1,64,256,256]{3,2,1,0:T(8,128)(2,1)} async-done(((bf16[1,64,32,256]{3,2,1,0:T(8,128)(2,1)}), bf16[1,64,256,256]{3,2,1,0:T(8,128)(2,1)}) %all-gather.3.cloned.1.call-update) | async-done | bytes 8388624 | tf_op jit(solution)/shard_map/all_gather | solution.py:174
  137.9 2.8 select_bitcast_fusion.1
  141.7 2.5 fusion.30
  146.6 4.5 collective-permute-start
  151.1 2.8 fusion.78
  155.8 2.7 fusion.76
  158.5 7.6 %concatenate.75 = bf16[64,32,820]{2,1,0:T(8,128)(2,1)} concatenate(bf16[64,32,164]{2,1,0:T(8,128)(2,1)} %get-tuple-element.86, bf16[64,32,164]{2,1,0:T(8,128)(2,1)} %get-tuple-element.87, bf16[64,32,128]{2,1,0:T(8,128)(2,1)S(1)} %bitcast.177, bf16[64,32,36]{2,1,0:T(8,128)(2,1)S(1)} %copy.20, bf16[64,32,164]{2,1,0:T(8,128)(2,1)S(1)} %get-tuple-element.56, ...), dimensions={2} | concatenate | bytes 6717440 | tf_op jit(solution)/shard_map/concatenate | solution.py:46
  166.1 4.4 fusion.34
  172.5 5.6 %collective-permute-start.2 = (bf16[64,2,128]{2,1,0:T(2,128)(2,1)}, bf16[64,2,128]{2,1,0:T(2,128)(2,1)}, u32[]{:S(2)}, u32[]{:S(2)}) collective-permute-start(bf16[64,2,128]{2,1,0:T(2,128)(2,1)} %get-tuple-element.78), channel_id=1, source_target_pairs={{0,1},{1,2},{2,3},{3,4},{4,5},{5,6},{6,7},{8,9},{9,10},{10,11},{11... | collective-permute-start | bytes 98312 | tf_op jit(solution)/shard_map/ppermute | solution.py:18
  201.7 7.6 %concatenate.90 = bf16[2048,820]{1,0:T(8,128)(2,1)} concatenate(bf16[2048,164]{1,0:T(8,128)(2,1)} %bitcast.185, bf16[2048,164]{1,0:T(8,128)(2,1)} %bitcast.186, bf16[2048,128]{1,0:T(8,128)(2,1)S(1)} %bitcast.178, bf16[2048,36]{1,0:T(8,128)(2,1)S(1)} %bitcast.173, bf16[2048,164]{1,0:T(8,128)(2,1)S(1)} %bitcast.184, bf16[2048,164]{1,0:T(8,128)(2,1)S(1)} %bitcast.183), dimensions={1} | concatenate | bytes 6717440 | tf_op jit(solution)/shard_map/concatenate | solution.py:46
  209.3 6.0 %copy.32 = bf16[820,2048]{1,0:T(8,128)(2,1)} copy(bf16[820,2048]{0,1:T(8,128)(2,1)} %bitcast.182) | data formatting | bytes 6717440 | tf_op jit(solution)/shard_map/dot_general | solution.py:73
  215.4 4.3 reshape.193
  221.2 2.8 fusion.75
  224.0 8.0 %concatenate.79 = bf16[64,32,820]{2,1,0:T(8,128)(2,1)} concatenate(bf16[64,32,164]{2,1,0:T(8,128)(2,1)} %get-tuple-element.54, bf16[64,32,164]{2,1,0:T(8,128)(2,1)} %get-tuple-element.53, bf16[64,32,164]{2,1,0:T(8,128)(2,1)} %get-tuple-element.52, bf16[64,32,164]{2,1,0:T(8,128)(2,1)S(1)} %get-tuple-element.51, bf16[64,32,164]{2,1,0:T(8,128)(2,1)S(1)} %get-tuple-element.50), dimensions={2} | concatenate | bytes 6717440 | tf_op jit(solution)/shard_map/concatenate | solution.py:46
  232.0 3.4 fusion.17
  239.0 2.4 pad_slice_fusion.3
  242.4 8.3 %concatenate.81 = bf16[64,32,820]{2,1,0:T(8,128)(2,1)} concatenate(bf16[64,32,164]{2,1,0:T(8,128)(2,1)} %get-tuple-element.73, bf16[64,32,164]{2,1,0:T(8,128)(2,1)} %get-tuple-element.71, bf16[64,32,128]{2,1,0:T(8,128)(2,1)} %copy-done.22, bf16[64,32,36]{2,1,0:T(8,128)(2,1)S(1)} %copy.20, bf16[64,32,164]{2,1,0:T(8,128)(2,1)} %get-tuple-element.72, ...), dimensions={2} | concatenate | bytes 6717440 | tf_op jit(solution)/shard_map/concatenate | solution.py:46
  250.6 4.5 fusion.16
  255.2 3.3 fusion.44
  261.1 8.5 %concatenate.83 = bf16[64,32,820]{2,1,0:T(8,128)(2,1)} concatenate(bf16[64,32,164]{2,1,0:T(8,128)(2,1)} %get-tuple-element.69, bf16[64,32,164]{2,1,0:T(8,128)(2,1)} %get-tuple-element.68, bf16[64,32,164]{2,1,0:T(8,128)(2,1)} %get-tuple-element.67, bf16[64,32,164]{2,1,0:T(8,128)(2,1)} %get-tuple-element.66, bf16[64,32,164]{2,1,0:T(8,128)(2,1)} %get-tuple-element.65), dimensions={2} | concatenate | bytes 6717440 | tf_op jit(solution)/shard_map/concatenate | solution.py:46
  269.7 5.3 %fusion.48 = (bf16[64,32,128]{2,1,0:T(8,128)(2,1)S(1)}, bf16[64,32,128]{2,1,0:T(8,128)(2,1)S(1)}, bf16[1,64,32,128]{3,2,1,0:T(8,128)(2,1)}) fusion(f32[64,32,128]{2,1,0:T(8,128)} %fusion.16, bf16[64,32,128]{2,1,0:T(8,128)(2,1)S(1)} %copy-done.23, f32[1,64,32,128]{3,2,1,0:T(8,128)} %param.14, bf16[1,3,64,32,128]{4,3,2,1,0:T(8,128)(2,1)} %param.12, ...), kind=kOutput, calls=%fused_computation.80 | convolution fusion | flops 434634752 | bytes 8287232 | tf_op jit(solution)/shard_map/dot_general | solution.py:59
  290.7 6.0 %copy.35 = bf16[820,2048]{1,0:T(8,128)(2,1)} copy(bf16[820,2048]{0,1:T(8,128)(2,1)} %bitcast.181) | data formatting | bytes 6717440 | tf_op jit(solution)/shard_map/dot_general | solution.py:73
  296.7 4.2 reshape.208
  300.8 6.0 %copy.34 = bf16[820,2048]{1,0:T(8,128)(2,1)} copy(bf16[820,2048]{0,1:T(8,128)(2,1)} %bitcast.180) | data formatting | bytes 6717440 | tf_op jit(solution)/shard_map/dot_general | solution.py:73
  306.8 4.4 reshape.204
  311.3 4.0 convolution_bitcast_fusion.1
  317.1 6.0 %copy.33 = bf16[820,2048]{1,0:T(8,128)(2,1)} copy(bf16[820,2048]{0,1:T(8,128)(2,1)} %bitcast.174) | data formatting | bytes 6717440 | tf_op jit(solution)/shard_map/dot_general | solution.py:73
  323.1 4.2 reshape.201
  328.6 4.5 collective-permute-start.4
  350.9 5.7 %collective-permute-start.6 = (f32[64,2,128]{2,1,0:T(2,128)S(1)}, f32[64,2,128]{2,1,0:T(2,128)S(1)}, u32[]{:S(2)}, u32[]{:S(2)}) collective-permute-start(f32[64,2,128]{2,1,0:T(2,128)S(1)} %add_add_fusion.2), channel_id=1, source_target_pairs={{0,1},{1,2},{2,3},{3,4},{4,5},{5,6},{6,7},{8,9},{9,10},{10,11},{11... | collective-permute-start | bytes 196616 | tf_op jit(solution)/shard_map/ppermute | solution.py:18
  360.4 122.4 %all-reduce.38.cloned.1.call-done = f32[2,3,5,164,128]{4,3,2,1,0:T(8,128)} async-done(((f32[2,3,5,164,128]{4,3,2,1,0:T(8,128)}), f32[2,3,5,164,128]{4,3,2,1,0:T(8,128)}) %all-reduce.38.cloned.1.call-update) | async-done | bytes 2519056 | tf_op jit(solution)/shard_map/psum | solution.py:216
  482.8 4.5 copy.36
  (201 shorter events, 79.9 us)
Async XLA Ops:
  7.2 133.5 %copy-start = (bf16[1,64,32,256]{3,2,1,0:T(8,128)(2,1)S(1)}, bf16[1,64,32,256]{3,2,1,0:T(8,128)(2,1)}, u32[]{:S(2)}) copy-start(bf16[1,64,32,256]{3,2,1,0:T(8,128)(2,1)} %param.8) | copy-start | bytes 3145732
  7.2 130.7 %all-gather.3.cloned.1.call-start = ((), (), s32[]{:S(2)}) async-start(), calls=%async_computation.1 | async-start | bytes 9437184 | tf_op jit(solution)/shard_map/all_gather | solution.py:174
  7.9 474.8 %all-reduce.38.cloned.1.call-start = ((), (), s32[]{:S(2)}) async-start(), calls=%async_computation | async-start | bytes 5160960 | tf_op jit(solution)/shard_map/psum | solution.py:216
  141.7 9.4 %copy-start.17 = (bf16[2,3,5,164,128]{4,0,3,2,1:T(2,128)(2,1)S(1)}, bf16[2,3,5,164,128]{4,0,3,2,1:T(2,128)(2,1)}, u32[]{:S(2)}) copy-start(bf16[2,3,5,164,128]{4,0,3,2,1:T(2,128)(2,1)} %param.13) | copy-start | bytes 3778564
  145.3 9.6 %collective-permute-start.1 = (bf16[64,2,164]{2,1,0:T(2,128)(2,1)S(1)}, bf16[64,2,164]{2,1,0:T(2,128)(2,1)S(1)}, u32[]{:S(2)}, u32[]{:S(2)}) collective-permute-start(bf16[64,2,164]{2,1,0:T(2,128)(2,1)S(1)} %get-tuple-element.76), channel_id=1, source_target_pairs={{1,0},{2,1},{3,2},{4,3},{5,4},{6,5},{7,6},{9,8},{10,9},{11,10},{12... | collective-permute-start | bytes 125960 | tf_op jit(solution)/shard_map/ppermute | solution.py:21
  146.6 8.3 %collective-permute-start = (bf16[64,2,164]{2,1,0:T(2,128)(2,1)S(1)}, bf16[64,2,164]{2,1,0:T(2,128)(2,1)S(1)}, u32[]{:S(2)}, u32[]{:S(2)}) collective-permute-start(bf16[64,2,164]{2,1,0:T(2,128)(2,1)S(1)} %get-tuple-element.77), channel_id=1, source_target_pairs={{0,1},{1,2},{2,3},{3,4},{4,5},{5,6},{6,7},{8,9},{9,10},{10,11},{11... | collective-permute-start | bytes 125960 | tf_op jit(solution)/shard_map/ppermute | solution.py:18
  166.1 12.1 %copy-start.34 = (bf16[1,1,5,164,128]{4,0,3,2,1:T(2,128)(2,1)S(1)}, bf16[1,1,5,164,128]{4,0,3,2,1:T(2,128)(2,1)}, u32[]{:S(2)}) copy-start(bf16[1,1,5,164,128]{4,0,3,2,1:T(2,128)(2,1)} %get-tuple-element.59) | copy-start | bytes 629764
  166.1 12.8 %copy-start.33 = (bf16[1,1,5,164,128]{4,0,3,2,1:T(2,128)(2,1)S(1)}, bf16[1,1,5,164,128]{4,0,3,2,1:T(2,128)(2,1)}, u32[]{:S(2)}) copy-start(bf16[1,1,5,164,128]{4,0,3,2,1:T(2,128)(2,1)} %get-tuple-element.60) | copy-start | bytes 629764
  170.6 12.0 %copy-start.46 = (bf16[64,32,128]{2,1,0:T(8,128)(2,1)}, bf16[64,32,128]{2,1,0:T(8,128)(2,1)S(1)}, u32[]{:S(2)}) copy-start(bf16[64,32,128]{2,1,0:T(8,128)(2,1)S(1)} %get-tuple-element.80) | copy-start | bytes 1572868
  170.6 9.8 %copy-start.32 = (bf16[1,1,5,164,128]{4,0,3,2,1:T(2,128)(2,1)S(1)}, bf16[1,1,5,164,128]{4,0,3,2,1:T(2,128)(2,1)}, u32[]{:S(2)}) copy-start(bf16[1,1,5,164,128]{4,0,3,2,1:T(2,128)(2,1)} %get-tuple-element.61) | copy-start | bytes 629764
  170.6 11.2 %copy-start.31 = (bf16[1,1,5,164,128]{4,0,3,2,1:T(2,128)(2,1)S(1)}, bf16[1,1,5,164,128]{4,0,3,2,1:T(2,128)(2,1)}, u32[]{:S(2)}) copy-start(bf16[1,1,5,164,128]{4,0,3,2,1:T(2,128)(2,1)} %get-tuple-element.62) | copy-start | bytes 629764
  171.2 48.4 %collective-permute-start.3 = (bf16[64,2,128]{2,1,0:T(2,128)(2,1)}, bf16[64,2,128]{2,1,0:T(2,128)(2,1)S(1)}, u32[]{:S(2)}, u32[]{:S(2)}) collective-permute-start(bf16[64,2,128]{2,1,0:T(2,128)(2,1)} %get-tuple-element.79), channel_id=1, source_target_pairs={{1,0},{2,1},{3,2},{4,3},{5,4},{6,5},{7,6},{9,8},{10,9},{11,10},{12... | collective-permute-start | bytes 98312 | tf_op jit(solution)/shard_map/ppermute | solution.py:21
  172.5 47.1 %collective-permute-start.2 = (bf16[64,2,128]{2,1,0:T(2,128)(2,1)}, bf16[64,2,128]{2,1,0:T(2,128)(2,1)}, u32[]{:S(2)}, u32[]{:S(2)}) collective-permute-start(bf16[64,2,128]{2,1,0:T(2,128)(2,1)} %get-tuple-element.78), channel_id=1, source_target_pairs={{0,1},{1,2},{2,3},{3,4},{4,5},{5,6},{6,7},{8,9},{9,10},{10,11},{11... | collective-permute-start | bytes 98312 | tf_op jit(solution)/shard_map/ppermute | solution.py:18
  178.2 5.0 %copy-start.30 = (bf16[1,1,5,164,128]{4,0,3,2,1:T(2,128)(2,1)S(1)}, bf16[1,1,5,164,128]{4,0,3,2,1:T(2,128)(2,1)}, u32[]{:S(2)}) copy-start(bf16[1,1,5,164,128]{4,0,3,2,1:T(2,128)(2,1)} %copy-done.29) | copy-start | bytes 629764
  179.0 5.0 %copy-start.28 = (bf16[1,1,5,164,128]{4,0,3,2,1:T(2,128)(2,1)S(1)}, bf16[1,1,5,164,128]{4,0,3,2,1:T(2,128)(2,1)}, u32[]{:S(2)}) copy-start(bf16[1,1,5,164,128]{4,0,3,2,1:T(2,128)(2,1)} %get-tuple-element.64) | copy-start | bytes 629764
  224.0 8.0 %copy-start.45 = (bf16[820,128,1]{1,0,2:T(8,128)(2,1)S(1)}, bf16[820,128,1]{1,0,2:T(8,128)(2,1)}, u32[]{:S(2)}) copy-start(bf16[820,128,1]{1,0,2:T(8,128)(2,1)} %reshape.226) | copy-start | bytes 629764
  237.9 47.4 %copy-start.11 = (f32[64,32,128]{2,1,0:T(8,128)}, f32[64,32,128]{2,1,0:T(8,128)S(1)}, u32[]{:S(2)}) copy-start(f32[64,32,128]{2,1,0:T(8,128)S(1)} %get-tuple-element.83) | copy-start | bytes 3145732
  250.6 4.5 copy-start.8
  250.6 4.5 copy-start.23
  250.6 4.5 copy-start.58
  269.7 6.1 %copy-start.52 = (bf16[5,128,128]{2,1,0:T(8,128)(2,1)S(1)}, bf16[5,128,128]{2,1,0:T(8,128)(2,1)}, u32[]{:S(2)}) copy-start(bf16[5,128,128]{2,1,0:T(8,128)(2,1)} %slice.398) | copy-start | bytes 491524
  275.0 5.6 %copy-start.39 = (bf16[64,32,128]{2,1,0:T(8,128)(2,1)}, bf16[64,32,128]{2,1,0:T(8,128)(2,1)S(1)}, u32[]{:S(2)}) copy-start(bf16[64,32,128]{2,1,0:T(8,128)(2,1)S(1)} %get-tuple-element.47) | copy-start | bytes 1572868
  323.1 10.1 %copy-start.48 = (bf16[5,128,128]{2,1,0:T(8,128)(2,1)S(1)}, bf16[5,128,128]{2,1,0:T(8,128)(2,1)}, u32[]{:S(2)}) copy-start(bf16[5,128,128]{2,1,0:T(8,128)(2,1)} %slice.423) | copy-start | bytes 491524
  327.3 14.4 %collective-permute-start.5 = (f32[64,2,128]{2,1,0:T(2,128)}, f32[64,2,128]{2,1,0:T(2,128)S(1)}, u32[]{:S(2)}, u32[]{:S(2)}) collective-permute-start(f32[64,2,128]{2,1,0:T(2,128)} %get-tuple-element.26), channel_id=1, source_target_pairs={{1,0},{2,1},{3,2},{4,3},{5,4},{6,5},{7,6},{9,8},{10,9},{11,10},{12... | collective-permute-start | bytes 196616 | tf_op jit(solution)/shard_map/ppermute | solution.py:21
  328.6 13.1 %collective-permute-start.4 = (f32[64,2,128]{2,1,0:T(2,128)S(1)}, f32[64,2,128]{2,1,0:T(2,128)S(1)}, u32[]{:S(2)}, u32[]{:S(2)}) collective-permute-start(f32[64,2,128]{2,1,0:T(2,128)S(1)} %get-tuple-element.25), channel_id=1, source_target_pairs={{0,1},{1,2},{2,3},{3,4},{4,5},{5,6},{6,7},{8,9},{9,10},{10,11},{11... | collective-permute-start | bytes 196616 | tf_op jit(solution)/shard_map/ppermute | solution.py:18
  349.4 9.0 %collective-permute-start.7 = (f32[64,2,128]{2,1,0:T(2,128)S(1)}, f32[64,2,128]{2,1,0:T(2,128)S(1)}, u32[]{:S(2)}, u32[]{:S(2)}) collective-permute-start(f32[64,2,128]{2,1,0:T(2,128)S(1)} %add_add_fusion.1), channel_id=1, source_target_pairs={{1,0},{2,1},{3,2},{4,3},{5,4},{6,5},{7,6},{9,8},{10,9},{11,10},{12... | collective-permute-start | bytes 196616 | tf_op jit(solution)/shard_map/ppermute | solution.py:21
  350.8 8.0 %copy-start.12 = (f32[64,32,128]{2,1,0:T(8,128)S(1)}, f32[64,32,128]{2,1,0:T(8,128)}, u32[]{:S(2)}) copy-start(f32[64,32,128]{2,1,0:T(8,128)} %copy-done.11) | copy-start | bytes 3145732
  350.9 8.0 %copy-start.14 = (f32[64,32,128]{2,1,0:T(8,128)S(1)}, f32[64,32,128]{2,1,0:T(8,128)}, u32[]{:S(2)}) copy-start(f32[64,32,128]{2,1,0:T(8,128)} %copy-done.13) | copy-start | bytes 3145732
  350.9 7.9 %copy-start.16 = (f32[64,36,128]{2,1,0:T(8,128)S(1)}, f32[64,36,128]{2,1,0:T(8,128)}, u32[]{:S(2)}) copy-start(f32[64,36,128]{2,1,0:T(8,128)} %pad_add_fusion) | copy-start | bytes 3538948
  350.9 7.9 %copy-start.26 = (f32[64,32,128]{2,1,0:T(8,128)S(1)}, f32[64,32,128]{2,1,0:T(8,128)}, u32[]{:S(2)}) copy-start(f32[64,32,128]{2,1,0:T(8,128)} %get-tuple-element.81) | copy-start | bytes 3145732
  350.9 7.9 %collective-permute-start.6 = (f32[64,2,128]{2,1,0:T(2,128)S(1)}, f32[64,2,128]{2,1,0:T(2,128)S(1)}, u32[]{:S(2)}, u32[]{:S(2)}) collective-permute-start(f32[64,2,128]{2,1,0:T(2,128)S(1)} %add_add_fusion.2), channel_id=1, source_target_pairs={{0,1},{1,2},{2,3},{3,4},{4,5},{5,6},{6,7},{8,9},{9,10},{10,11},{11... | collective-permute-start | bytes 196616 | tf_op jit(solution)/shard_map/ppermute | solution.py:18
  358.8 128.4 %copy-start.1 = (bf16[1,64,32,256]{3,2,1,0:T(8,128)(2,1)S(1)}, bf16[1,64,32,256]{3,2,1,0:T(8,128)(2,1)}, u32[]{:S(2)}) copy-start(bf16[1,64,32,256]{3,2,1,0:T(8,128)(2,1)} %param.8) | copy-start | bytes 3145732
  (38 other events, 80.8 us)
Sparse Core Ops, SparseCore 0:
  10.2 127.6 all-gather.2
  346.7 136.0 all-reduce.37
where the time goes:
time: 504 us; the launch traced here: 494 us
  waiting for transfers between devices  253 us (50%)
  local copies, waits for them, and re-layouts  141 us (28%)
  matrix products  41.8 us (8%)
  starting transfers between devices  25.7 us (5%)
  other arithmetic  17.8 us (4%)
  between operations  15.8 us (3%)
    all_gather x1, waiting for transfers between devices, on_device(): shards = lax.all_gather(right_block, 'blk', axis=1, tiled=True)  129 us
    psum x1, waiting for transfers between devices, on_device(): lax.psum(jnp.stack([first_grads, second_grads]), ('pair', 'blk'))  122 us
    concatenate x5, local copies, waits for them, and re-layouts, tap_stack(): jnp.concatenate([lax.slice_in_dim(padded, tap_id, tap_id + extent, axis=a...  40 us
    dot_general x4, local copies, waits for them, and re-layouts, conv_weight_grad(): lax.dot_general(flat_taps, flat_deltas, (((0,), (0,)), ((), ())), preferr...  24 us
    dot_general x6, matrix products, conv_apply(): jnp.dot(flat_taps, weight_taps.reshape(kernel_len * in_chan, out_chan), p...  23.4 us
    unnamed x133, local copies, waits for them, and re-layouts  22.1 us
    ppermute x4, starting transfers between devices, with_halo(): lax.ppermute(lax.slice_in_dim(block, block.shape[dim] - width, None, axis...  20.5 us
    another operation x4, local copies, waits for them, and re-layouts  17 us
  transfers between devices with their start and end apart: 10, of which 3 were waited for; matrix products, arithmetic and copies ran while one was open for 11% of the time, Pallas kernels for 0%

commit v1 on v0

--- a/solution.py
+++ b/solution.py
@@ -171,7 +171,29 @@
     empty_block = jnp.zeros_like(right_block)
     low_id = stripe - offset - 1
     high_id = stripe - offset
-    shards = lax.all_gather(right_block, "blk", axis=1, tiled=True)
+    z_new, base_arr, block_last = (lax.psum(1, "blk"), lax.axis_index("blk"), right_block.shape[1])
+    fields = []
+    for dev_j, k0 in enumerate(right_block.shape):
+        fields.append(k0 * z_new if dev_j == 1 else k0)
+    mid_arr = jnp.zeros(fields, right_block.dtype)
+    shards = lax.dynamic_update_slice_in_dim(mid_arr, right_block, base_arr * block_last, axis=1)
+    top = f_now = right_block
+    for h in range(1, z_new // 2 + 1):
+        in_order = []
+        for dev_j in range(z_new):
+            in_order.append((dev_j, (dev_j + 1) % z_new))
+        top = lax.ppermute(top, "blk", in_order)
+        shards = lax.dynamic_update_slice_in_dim(
+            shards, top, (base_arr - h) % z_new * block_last, axis=1
+        )
+        if 2 * h < z_new:
+            parts_seen = []
+            for dev_j in range(z_new):
+                parts_seen.append((dev_j, (dev_j - 1) % z_new))
+            f_now = lax.ppermute(f_now, "blk", parts_seen)
+            shards = lax.dynamic_update_slice_in_dim(
+                shards, f_now, (base_arr + h) % z_new * block_last, axis=1
+            )
     shard_cols = shards.shape[1]
 
     def pick_one(slot_block, block_id):

time: 504 us -> 537 us (1.065)
  starting transfers between devices: 25.7 us -> 44.7 us
  waiting for transfers between devices: 253 us -> 264 us
    ppermute x0 -> x7, waiting for transfers between devices: none -> 140 us  [the longest x4 140 us: on_device(): top = lax.ppermute(top, 'blk', in_order)]
    all_gather x1 -> x0, waiting for transfers between devices: 129 us -> none  [on_device(): shards = lax.all_gather(right_block, 'blk', axis=1, tiled=True)]
    ppermute x0 -> x7, starting transfers between devices: none -> 19.6 us  [the longest x4 10.5 us: on_device(): top = lax.ppermute(top, 'blk', in_order)]
    dynamic_update_slice x0 -> x8, local copies, waits for them, and re-layouts: none -> 5.65 us  [the longest x4 2.82 us: on_device(): lax.dynamic_update_slice_in_dim(shards, top, (base_arr - h) % z_new * blo...]
    unnamed x133 -> x135, local copies, waits for them, and re-layouts: 22.1 us -> 20.9 us
  transfers between devices with their start and end apart: 10 -> 16, of which waited for: 3 -> 6; matrix products, arithmetic and copies ran while one was open for 11% -> 12% of each run, Pallas kernels for 0% -> 0%
where the time goes in v1:
time: 537 us; the launch traced here: 529 us
  waiting for transfers between devices  264 us (49%)
  local copies, waits for them, and re-layouts  146 us (27%)
  starting transfers between devices  44.7 us (8%)
  matrix products  41.8 us (8%)
  other arithmetic  16.2 us (3%)
  between operations  15.8 us (3%)
    ppermute x4, waiting for transfers between devices, on_device(): top = lax.ppermute(top, 'blk', in_order)  140 us
    psum x1, waiting for transfers between devices, on_device(): lax.psum(jnp.stack([first_grads, second_grads]), ('pair', 'blk'))  123 us
    concatenate x5, local copies, waits for them, and re-layouts, tap_stack(): jnp.concatenate([lax.slice_in_dim(padded, tap_id, tap_id + extent, axis=a...  40 us
    dot_general x4, local copies, waits for them, and re-layouts, conv_weight_grad(): lax.dot_general(flat_taps, flat_deltas, (((0,), (0,)), ((), ())), preferr...  24.1 us
    dot_general x6, matrix products, conv_apply(): jnp.dot(flat_taps, weight_taps.reshape(kernel_len * in_chan, out_chan), p...  23.4 us
    unnamed x135, local copies, waits for them, and re-layouts  20.9 us
    ppermute x4, starting transfers between devices, with_halo(): lax.ppermute(lax.slice_in_dim(block, block.shape[dim] - width, None, axis...  19.9 us
    another operation x4, local copies, waits for them, and re-layouts  17.2 us
  transfers between devices with their start and end apart: 16, of which 6 were waited for; matrix products, arithmetic and copies ran while one was open for 12% of the time, Pallas kernels for 0%

profile of v1, /device:TPU:0, one launch (start us, length us, event | category | flops | bytes accessed | tf_op | source)
XLA Modules:
  0.0 528.9 jit_solution(12100564626631081212)
XLA Ops:
  10.2 3.1 collective-permute-start.1
  13.4 42.1 %collective-permute-done = bf16[64,32,256]{2,1,0:T(8,128)(2,1)S(1)} collective-permute-done((bf16[64,32,256]{2,1,0:T(8,128)(2,1)}, bf16[64,32,256]{2,1,0:T(8,128)(2,1)S(1)}, u32[]{:S(2)}, u32[]{:S(2)}) %collective-permute-start) | collective-permute-done | bytes 1048608 | tf_op jit(solution)/shard_map/ppermute | solution.py:185
  57.8 3.0 collective-permute-start.3
  60.9 41.0 %collective-permute-done.2 = bf16[64,32,256]{2,1,0:T(8,128)(2,1)} collective-permute-done((bf16[64,32,256]{2,1,0:T(8,128)(2,1)S(1)}, bf16[64,32,256]{2,1,0:T(8,128)(2,1)}, u32[]{:S(2)}, u32[]{:S(2)}) %collective-permute-start.2) | collective-permute-done | bytes 1048608 | tf_op jit(solution)/shard_map/ppermute | solution.py:185
  104.4 3.0 collective-permute-start.5
  108.2 39.8 %collective-permute-done.4 = bf16[64,32,256]{2,1,0:T(8,128)(2,1)} collective-permute-done((bf16[64,32,256]{2,1,0:T(8,128)(2,1)}, bf16[64,32,256]{2,1,0:T(8,128)(2,1)}, u32[]{:S(2)}, u32[]{:S(2)}) %collective-permute-start.4) | collective-permute-done | bytes 1048608 | tf_op jit(solution)/shard_map/ppermute | solution.py:185
  157.1 17.2 %collective-permute-done.6 = bf16[64,32,256]{2,1,0:T(8,128)(2,1)S(1)} collective-permute-done((bf16[64,32,256]{2,1,0:T(8,128)(2,1)}, bf16[64,32,256]{2,1,0:T(8,128)(2,1)S(1)}, u32[]{:S(2)}, u32[]{:S(2)}) %collective-permute-start.6) | collective-permute-done | bytes 1048608 | tf_op jit(solution)/shard_map/ppermute | solution.py:185
  181.5 5.1 collective-permute-start.7
  193.9 7.6 %concatenate.75 = bf16[64,32,820]{2,1,0:T(8,128)(2,1)} concatenate(bf16[64,32,164]{2,1,0:T(8,128)(2,1)} %get-tuple-element.86, bf16[64,32,164]{2,1,0:T(8,128)(2,1)} %get-tuple-element.87, bf16[64,32,128]{2,1,0:T(8,128)(2,1)S(1)} %bitcast.175, bf16[64,32,36]{2,1,0:T(8,128)(2,1)S(1)} %copy.20, bf16[64,32,164]{2,1,0:T(8,128)(2,1)S(1)} %get-tuple-element.56, ...), dimensions={2} | concatenate | bytes 6717440 | tf_op jit(solution)/shard_map/concatenate | solution.py:46
  201.5 4.4 fusion.34
  208.0 5.3 %collective-permute-start.9 = (bf16[64,2,128]{2,1,0:T(2,128)(2,1)}, bf16[64,2,128]{2,1,0:T(2,128)(2,1)}, u32[]{:S(2)}, u32[]{:S(2)}) collective-permute-start(bf16[64,2,128]{2,1,0:T(2,128)(2,1)} %get-tuple-element.78), channel_id=1, source_target_pairs={{0,1},{1,2},{2,3},{3,4},{4,5},{5,6},{6,7},{8,9},{9,10},{10,11},{11... | collective-permute-start | bytes 98312 | tf_op jit(solution)/shard_map/ppermute | solution.py:18
  236.8 7.6 %concatenate.90 = bf16[2048,820]{1,0:T(8,128)(2,1)} concatenate(bf16[2048,164]{1,0:T(8,128)(2,1)} %bitcast.183, bf16[2048,164]{1,0:T(8,128)(2,1)} %bitcast.184, bf16[2048,128]{1,0:T(8,128)(2,1)S(1)} %bitcast.176, bf16[2048,36]{1,0:T(8,128)(2,1)S(1)} %bitcast.171, bf16[2048,164]{1,0:T(8,128)(2,1)S(1)} %bitcast.182, bf16[2048,164]{1,0:T(8,128)(2,1)S(1)} %bitcast.181), dimensions={1} | concatenate | bytes 6717440 | tf_op jit(solution)/shard_map/concatenate | solution.py:46
  244.4 6.0 %copy.32 = bf16[820,2048]{1,0:T(8,128)(2,1)} copy(bf16[820,2048]{0,1:T(8,128)(2,1)} %bitcast.180) | data formatting | bytes 6717440 | tf_op jit(solution)/shard_map/dot_general | solution.py:73
  250.4 4.2 reshape.193
  259.1 8.0 %concatenate.79 = bf16[64,32,820]{2,1,0:T(8,128)(2,1)} concatenate(bf16[64,32,164]{2,1,0:T(8,128)(2,1)} %get-tuple-element.54, bf16[64,32,164]{2,1,0:T(8,128)(2,1)} %get-tuple-element.53, bf16[64,32,164]{2,1,0:T(8,128)(2,1)} %get-tuple-element.52, bf16[64,32,164]{2,1,0:T(8,128)(2,1)S(1)} %get-tuple-element.51, bf16[64,32,164]{2,1,0:T(8,128)(2,1)S(1)} %get-tuple-element.50), dimensions={2} | concatenate | bytes 6717440 | tf_op jit(solution)/shard_map/concatenate | solution.py:46
  267.0 3.4 fusion.17
  277.3 8.3 %concatenate.81 = bf16[64,32,820]{2,1,0:T(8,128)(2,1)} concatenate(bf16[64,32,164]{2,1,0:T(8,128)(2,1)} %get-tuple-element.73, bf16[64,32,164]{2,1,0:T(8,128)(2,1)} %get-tuple-element.71, bf16[64,32,128]{2,1,0:T(8,128)(2,1)} %copy-done.22, bf16[64,32,36]{2,1,0:T(8,128)(2,1)S(1)} %copy.20, bf16[64,32,164]{2,1,0:T(8,128)(2,1)} %get-tuple-element.72, ...), dimensions={2} | concatenate | bytes 6717440 | tf_op jit(solution)/shard_map/concatenate | solution.py:46
  285.6 4.5 fusion.16
  290.1 3.3 fusion.44
  296.1 8.6 %concatenate.83 = bf16[64,32,820]{2,1,0:T(8,128)(2,1)} concatenate(bf16[64,32,164]{2,1,0:T(8,128)(2,1)} %get-tuple-element.69, bf16[64,32,164]{2,1,0:T(8,128)(2,1)} %get-tuple-element.68, bf16[64,32,164]{2,1,0:T(8,128)(2,1)} %get-tuple-element.67, bf16[64,32,164]{2,1,0:T(8,128)(2,1)} %get-tuple-element.66, bf16[64,32,164]{2,1,0:T(8,128)(2,1)} %get-tuple-element.65), dimensions={2} | concatenate | bytes 6717440 | tf_op jit(solution)/shard_map/concatenate | solution.py:46
  304.7 5.3 %fusion.48 = (bf16[64,32,128]{2,1,0:T(8,128)(2,1)S(1)}, bf16[64,32,128]{2,1,0:T(8,128)(2,1)S(1)}, bf16[1,64,32,128]{3,2,1,0:T(8,128)(2,1)}) fusion(f32[64,32,128]{2,1,0:T(8,128)} %fusion.16, bf16[64,32,128]{2,1,0:T(8,128)(2,1)S(1)} %copy-done.23, f32[1,64,32,128]{3,2,1,0:T(8,128)} %param.14, bf16[1,3,64,32,128]{4,3,2,1,0:T(8,128)(2,1)} %param.12, ...), kind=kOutput, calls=%fused_computation.80 | convolution fusion | flops 434634752 | bytes 8287232 | tf_op jit(solution)/shard_map/dot_general | solution.py:59
  325.7 6.0 %copy.35 = bf16[820,2048]{1,0:T(8,128)(2,1)} copy(bf16[820,2048]{0,1:T(8,128)(2,1)} %bitcast.179) | data formatting | bytes 6717440 | tf_op jit(solution)/shard_map/dot_general | solution.py:73
  331.7 4.2 reshape.208
  335.9 6.0 %copy.34 = bf16[820,2048]{1,0:T(8,128)(2,1)} copy(bf16[820,2048]{0,1:T(8,128)(2,1)} %bitcast.178) | data formatting | bytes 6717440 | tf_op jit(solution)/shard_map/dot_general | solution.py:73
  341.9 4.6 reshape.204
  346.5 4.0 convolution_bitcast_fusion.1
  352.3 6.0 %copy.33 = bf16[820,2048]{1,0:T(8,128)(2,1)} copy(bf16[820,2048]{0,1:T(8,128)(2,1)} %bitcast.172) | data formatting | bytes 6717440 | tf_op jit(solution)/shard_map/dot_general | solution.py:73
  358.4 4.2 reshape.201
  363.9 4.5 collective-permute-start.11
  385.1 5.0 collective-permute-start.13
  393.9 123.5 %all-reduce.38.cloned.1.call-done = f32[2,3,5,164,128]{4,3,2,1,0:T(8,128)} async-done(((f32[2,3,5,164,128]{4,3,2,1,0:T(8,128)}), f32[2,3,5,164,128]{4,3,2,1,0:T(8,128)}) %all-reduce.38.cloned.1.call-update) | async-done | bytes 2519056 | tf_op jit(solution)/shard_map/psum | solution.py:238
  517.4 4.5 copy.36
  (223 shorter events, 109.7 us)
Async XLA Ops:
  7.2 168.4 %copy-start = (bf16[1,64,32,256]{3,2,1,0:T(8,128)(2,1)S(1)}, bf16[1,64,32,256]{3,2,1,0:T(8,128)(2,1)}, u32[]{:S(2)}) copy-start(bf16[1,64,32,256]{3,2,1,0:T(8,128)(2,1)} %param.8) | copy-start | bytes 3145732
  7.2 510.2 %all-reduce.38.cloned.1.call-start = ((), (), s32[]{:S(2)}) async-start(), calls=%async_computation | async-start | bytes 5160960 | tf_op jit(solution)/shard_map/psum | solution.py:238
  7.2 48.2 %collective-permute-start = (bf16[64,32,256]{2,1,0:T(8,128)(2,1)}, bf16[64,32,256]{2,1,0:T(8,128)(2,1)S(1)}, u32[]{:S(2)}, u32[]{:S(2)}) collective-permute-start(bf16[64,32,256]{2,1,0:T(8,128)(2,1)} %bitcast.191), channel_id=1, source_target_pairs={{0,1},{1,2},{2,3},{3,4},{4,5},{5,6},{6,7},{7,0},{8,9},{9,10},{10,1... | collective-permute-start | bytes 3145736 | tf_op jit(solution)/shard_map/ppermute | solution.py:185
  10.2 47.6 %collective-permute-start.1 = (bf16[64,32,256]{2,1,0:T(8,128)(2,1)}, bf16[64,32,256]{2,1,0:T(8,128)(2,1)S(1)}, u32[]{:S(2)}, u32[]{:S(2)}) collective-permute-start(bf16[64,32,256]{2,1,0:T(8,128)(2,1)} %bitcast.192), channel_id=1, source_target_pairs={{0,7},{1,0},{2,1},{3,2},{4,3},{5,4},{6,5},{7,6},{8,15},{9,8},{10,9... | collective-permute-start | bytes 3145736 | tf_op jit(solution)/shard_map/ppermute | solution.py:193
  55.5 46.4 %collective-permute-start.2 = (bf16[64,32,256]{2,1,0:T(8,128)(2,1)S(1)}, bf16[64,32,256]{2,1,0:T(8,128)(2,1)}, u32[]{:S(2)}, u32[]{:S(2)}) collective-permute-start(bf16[64,32,256]{2,1,0:T(8,128)(2,1)S(1)} %collective-permute-done), channel_id=1, source_target_pairs={{0,1},{1,2},{2,3},{3,4},{4,5},{5,6},{6,7},{7,0},{8,9},{9,10},{10,1... | collective-permute-start | bytes 3145736 | tf_op jit(solution)/shard_map/ppermute | solution.py:185
  57.8 46.6 %collective-permute-start.3 = (bf16[64,32,256]{2,1,0:T(8,128)(2,1)S(1)}, bf16[64,32,256]{2,1,0:T(8,128)(2,1)}, u32[]{:S(2)}, u32[]{:S(2)}) collective-permute-start(bf16[64,32,256]{2,1,0:T(8,128)(2,1)S(1)} %collective-permute-done.1), channel_id=1, source_target_pairs={{0,7},{1,0},{2,1},{3,2},{4,3},{5,4},{6,5},{7,6},{8,15},{9,8},{10,9... | collective-permute-start | bytes 3145736 | tf_op jit(solution)/shard_map/ppermute | solution.py:193
  101.8 46.2 %collective-permute-start.4 = (bf16[64,32,256]{2,1,0:T(8,128)(2,1)}, bf16[64,32,256]{2,1,0:T(8,128)(2,1)}, u32[]{:S(2)}, u32[]{:S(2)}) collective-permute-start(bf16[64,32,256]{2,1,0:T(8,128)(2,1)} %collective-permute-done.2), channel_id=1, source_target_pairs={{0,1},{1,2},{2,3},{3,4},{4,5},{5,6},{6,7},{7,0},{8,9},{9,10},{10,1... | collective-permute-start | bytes 3145736 | tf_op jit(solution)/shard_map/ppermute | solution.py:185
  104.4 51.4 %collective-permute-start.5 = (bf16[64,32,256]{2,1,0:T(8,128)(2,1)}, bf16[64,32,256]{2,1,0:T(8,128)(2,1)}, u32[]{:S(2)}, u32[]{:S(2)}) collective-permute-start(bf16[64,32,256]{2,1,0:T(8,128)(2,1)} %collective-permute-done.3), channel_id=1, source_target_pairs={{0,7},{1,0},{2,1},{3,2},{4,3},{5,4},{6,5},{7,6},{8,15},{9,8},{10,9... | collective-permute-start | bytes 3145736 | tf_op jit(solution)/shard_map/ppermute | solution.py:193
  108.2 43.3 %copy-start.45 = (bf16[1,64,32,256]{3,2,1,0:T(8,128)(2,1)S(1)}, bf16[1,64,32,256]{3,2,1,0:T(8,128)(2,1)}, u32[]{:S(2)}) copy-start(bf16[1,64,32,256]{3,2,1,0:T(8,128)(2,1)} %param.9) | copy-start | bytes 3145732
  148.0 26.3 %collective-permute-start.6 = (bf16[64,32,256]{2,1,0:T(8,128)(2,1)}, bf16[64,32,256]{2,1,0:T(8,128)(2,1)S(1)}, u32[]{:S(2)}, u32[]{:S(2)}) collective-permute-start(bf16[64,32,256]{2,1,0:T(8,128)(2,1)} %collective-permute-done.4), channel_id=1, source_target_pairs={{0,1},{1,2},{2,3},{3,4},{4,5},{5,6},{6,7},{7,0},{8,9},{9,10},{10,1... | collective-permute-start | bytes 3145736 | tf_op jit(solution)/shard_map/ppermute | solution.py:185
  176.6 9.9 %copy-start.17 = (bf16[2,3,5,164,128]{4,0,3,2,1:T(2,128)(2,1)S(1)}, bf16[2,3,5,164,128]{4,0,3,2,1:T(2,128)(2,1)}, u32[]{:S(2)}) copy-start(bf16[2,3,5,164,128]{4,0,3,2,1:T(2,128)(2,1)} %param.13) | copy-start | bytes 3778564
  180.2 10.1 %collective-permute-start.8 = (bf16[64,2,164]{2,1,0:T(2,128)(2,1)S(1)}, bf16[64,2,164]{2,1,0:T(2,128)(2,1)S(1)}, u32[]{:S(2)}, u32[]{:S(2)}) collective-permute-start(bf16[64,2,164]{2,1,0:T(2,128)(2,1)S(1)} %get-tuple-element.76), channel_id=1, source_target_pairs={{1,0},{2,1},{3,2},{4,3},{5,4},{6,5},{7,6},{9,8},{10,9},{11,10},{12... | collective-permute-start | bytes 125960 | tf_op jit(solution)/shard_map/ppermute | solution.py:21
  181.5 8.8 %collective-permute-start.7 = (bf16[64,2,164]{2,1,0:T(2,128)(2,1)S(1)}, bf16[64,2,164]{2,1,0:T(2,128)(2,1)S(1)}, u32[]{:S(2)}, u32[]{:S(2)}) collective-permute-start(bf16[64,2,164]{2,1,0:T(2,128)(2,1)S(1)} %get-tuple-element.77), channel_id=1, source_target_pairs={{0,1},{1,2},{2,3},{3,4},{4,5},{5,6},{6,7},{8,9},{9,10},{10,11},{11... | collective-permute-start | bytes 125960 | tf_op jit(solution)/shard_map/ppermute | solution.py:18
  201.5 11.7 %copy-start.34 = (bf16[1,1,5,164,128]{4,0,3,2,1:T(2,128)(2,1)S(1)}, bf16[1,1,5,164,128]{4,0,3,2,1:T(2,128)(2,1)}, u32[]{:S(2)}) copy-start(bf16[1,1,5,164,128]{4,0,3,2,1:T(2,128)(2,1)} %get-tuple-element.59) | copy-start | bytes 629764
  201.5 12.5 %copy-start.33 = (bf16[1,1,5,164,128]{4,0,3,2,1:T(2,128)(2,1)S(1)}, bf16[1,1,5,164,128]{4,0,3,2,1:T(2,128)(2,1)}, u32[]{:S(2)}) copy-start(bf16[1,1,5,164,128]{4,0,3,2,1:T(2,128)(2,1)} %get-tuple-element.60) | copy-start | bytes 629764
  206.0 13.1 %copy-start.47 = (bf16[64,32,128]{2,1,0:T(8,128)(2,1)}, bf16[64,32,128]{2,1,0:T(8,128)(2,1)S(1)}, u32[]{:S(2)}) copy-start(bf16[64,32,128]{2,1,0:T(8,128)(2,1)S(1)} %get-tuple-element.80) | copy-start | bytes 1572868
  206.0 9.5 %copy-start.32 = (bf16[1,1,5,164,128]{4,0,3,2,1:T(2,128)(2,1)S(1)}, bf16[1,1,5,164,128]{4,0,3,2,1:T(2,128)(2,1)}, u32[]{:S(2)}) copy-start(bf16[1,1,5,164,128]{4,0,3,2,1:T(2,128)(2,1)} %get-tuple-element.61) | copy-start | bytes 629764
  206.0 10.9 %copy-start.31 = (bf16[1,1,5,164,128]{4,0,3,2,1:T(2,128)(2,1)S(1)}, bf16[1,1,5,164,128]{4,0,3,2,1:T(2,128)(2,1)}, u32[]{:S(2)}) copy-start(bf16[1,1,5,164,128]{4,0,3,2,1:T(2,128)(2,1)} %get-tuple-element.62) | copy-start | bytes 629764
  206.0 12.3 %copy-start.30 = (bf16[1,1,5,164,128]{4,0,3,2,1:T(2,128)(2,1)S(1)}, bf16[1,1,5,164,128]{4,0,3,2,1:T(2,128)(2,1)}, u32[]{:S(2)}) copy-start(bf16[1,1,5,164,128]{4,0,3,2,1:T(2,128)(2,1)} %copy-done.29) | copy-start | bytes 629764
  206.7 48.0 %collective-permute-start.10 = (bf16[64,2,128]{2,1,0:T(2,128)(2,1)}, bf16[64,2,128]{2,1,0:T(2,128)(2,1)S(1)}, u32[]{:S(2)}, u32[]{:S(2)}) collective-permute-start(bf16[64,2,128]{2,1,0:T(2,128)(2,1)} %get-tuple-element.79), channel_id=1, source_target_pairs={{1,0},{2,1},{3,2},{4,3},{5,4},{6,5},{7,6},{9,8},{10,9},{11,10},{12... | collective-permute-start | bytes 98312 | tf_op jit(solution)/shard_map/ppermute | solution.py:21
  208.0 46.7 %collective-permute-start.9 = (bf16[64,2,128]{2,1,0:T(2,128)(2,1)}, bf16[64,2,128]{2,1,0:T(2,128)(2,1)}, u32[]{:S(2)}, u32[]{:S(2)}) collective-permute-start(bf16[64,2,128]{2,1,0:T(2,128)(2,1)} %get-tuple-element.78), channel_id=1, source_target_pairs={{0,1},{1,2},{2,3},{3,4},{4,5},{5,6},{6,7},{8,9},{9,10},{10,11},{11... | collective-permute-start | bytes 98312 | tf_op jit(solution)/shard_map/ppermute | solution.py:18
  259.1 8.0 %copy-start.46 = (bf16[820,128,1]{1,0,2:T(8,128)(2,1)S(1)}, bf16[820,128,1]{1,0,2:T(8,128)(2,1)}, u32[]{:S(2)}) copy-start(bf16[820,128,1]{1,0,2:T(8,128)(2,1)} %reshape.217) | copy-start | bytes 629764
  272.9 47.4 %copy-start.11 = (f32[64,32,128]{2,1,0:T(8,128)}, f32[64,32,128]{2,1,0:T(8,128)S(1)}, u32[]{:S(2)}) copy-start(f32[64,32,128]{2,1,0:T(8,128)S(1)} %get-tuple-element.83) | copy-start | bytes 3145732
  358.4 10.1 %copy-start.49 = (bf16[5,128,128]{2,1,0:T(8,128)(2,1)S(1)}, bf16[5,128,128]{2,1,0:T(8,128)(2,1)}, u32[]{:S(2)}) copy-start(bf16[5,128,128]{2,1,0:T(8,128)(2,1)} %slice.423) | copy-start | bytes 491524
  362.6 14.4 %collective-permute-start.12 = (f32[64,2,128]{2,1,0:T(2,128)}, f32[64,2,128]{2,1,0:T(2,128)S(1)}, u32[]{:S(2)}, u32[]{:S(2)}) collective-permute-start(f32[64,2,128]{2,1,0:T(2,128)} %get-tuple-element.26), channel_id=1, source_target_pairs={{1,0},{2,1},{3,2},{4,3},{5,4},{6,5},{7,6},{9,8},{10,9},{11,10},{12... | collective-permute-start | bytes 196616 | tf_op jit(solution)/shard_map/ppermute | solution.py:21
  363.9 13.1 %collective-permute-start.11 = (f32[64,2,128]{2,1,0:T(2,128)S(1)}, f32[64,2,128]{2,1,0:T(2,128)S(1)}, u32[]{:S(2)}, u32[]{:S(2)}) collective-permute-start(f32[64,2,128]{2,1,0:T(2,128)S(1)} %get-tuple-element.25), channel_id=1, source_target_pairs={{0,1},{1,2},{2,3},{3,4},{4,5},{5,6},{6,7},{8,9},{9,10},{10,11},{11... | collective-permute-start | bytes 196616 | tf_op jit(solution)/shard_map/ppermute | solution.py:18
  383.6 8.2 %collective-permute-start.14 = (f32[64,2,128]{2,1,0:T(2,128)S(1)}, f32[64,2,128]{2,1,0:T(2,128)S(1)}, u32[]{:S(2)}, u32[]{:S(2)}) collective-permute-start(f32[64,2,128]{2,1,0:T(2,128)S(1)} %add_add_fusion.1), channel_id=1, source_target_pairs={{1,0},{2,1},{3,2},{4,3},{5,4},{6,5},{7,6},{9,8},{10,9},{11,10},{12... | collective-permute-start | bytes 196616 | tf_op jit(solution)/shard_map/ppermute | solution.py:21
  385.1 7.3 %copy-start.12 = (f32[64,32,128]{2,1,0:T(8,128)S(1)}, f32[64,32,128]{2,1,0:T(8,128)}, u32[]{:S(2)}) copy-start(f32[64,32,128]{2,1,0:T(8,128)} %copy-done.11) | copy-start | bytes 3145732
  385.1 7.2 %copy-start.14 = (f32[64,32,128]{2,1,0:T(8,128)S(1)}, f32[64,32,128]{2,1,0:T(8,128)}, u32[]{:S(2)}) copy-start(f32[64,32,128]{2,1,0:T(8,128)} %copy-done.13) | copy-start | bytes 3145732
  385.1 7.2 %copy-start.16 = (f32[64,36,128]{2,1,0:T(8,128)S(1)}, f32[64,36,128]{2,1,0:T(8,128)}, u32[]{:S(2)}) copy-start(f32[64,36,128]{2,1,0:T(8,128)} %pad_add_fusion) | copy-start | bytes 3538948
  385.1 7.2 %collective-permute-start.13 = (f32[64,2,128]{2,1,0:T(2,128)S(1)}, f32[64,2,128]{2,1,0:T(2,128)S(1)}, u32[]{:S(2)}, u32[]{:S(2)}) collective-permute-start(f32[64,2,128]{2,1,0:T(2,128)S(1)} %add_add_fusion.2), channel_id=1, source_target_pairs={{0,1},{1,2},{2,3},{3,4},{4,5},{5,6},{6,7},{8,9},{9,10},{10,11},{11... | collective-permute-start | bytes 196616 | tf_op jit(solution)/shard_map/ppermute | solution.py:18
  392.4 129.5 %copy-start.1 = (bf16[1,64,32,256]{3,2,1,0:T(8,128)(2,1)S(1)}, bf16[1,64,32,256]{3,2,1,0:T(8,128)(2,1)}, u32[]{:S(2)}) copy-start(bf16[1,64,32,256]{3,2,1,0:T(8,128)(2,1)} %param.8) | copy-start | bytes 3145732
  (45 other events, 119.3 us)
Sparse Core Ops, SparseCore 0:
  380.9 136.3 all-reduce.37
